TPU v7x, 512 devices: a whole 4x8x8 slice. The times are simulated.
512 devices in a mesh: seq: 64 (over z, y), head: 8 (over x, core).
Axes of the slice: x: 4, y: 8, z: 8, core: 2. Of those that a mesh axis runs over, the one named last changes fastest.
Arguments:
- queries: bfloat16 [9216, 8192], P('seq', 'head'), may hold values from -24 to 24
- key_matrix: bfloat16 [9216, 1024], P('seq', 'head'), may hold values from -4 to 4
- value_matrix: bfloat16 [9216, 1024], P('seq', 'head'), may hold values from -6 to 6
- query_feature_weight: bfloat16 [128, 4096], P(None, 'head'), may hold values from -0.5 to 0.5
- key_feature_weight: bfloat16 [128, 512], P(None, 'head'), may hold values from -0.5 to 0.5
Outputs:
- student_out: bfloat16 [9216, 8192], P('seq', 'head')
- query_map_grad: float32 [128, 4096], P(None, 'head')
- key_weight_gradient: float32 [128, 512], P(None, 'head')
- transfer_loss: float32 [], replicated
All inputs are finite; a program needn't handle non-finite values.
Results may differ from a plain program's by a relative error of at most 0.008.
Values may be sent and summed in bfloat16 or wider, within the bound.
A program may use at most 128 MiB of HBM per device.

v0:
```python
import jax
import jax.numpy as jnp
from jax import lax
from jax.sharding import PartitionSpec as P

HEAD_SIZE = 128
GROUP_QUERIES = 8
HALF_FEATURES = 64
NEG_LARGE = -1e30


def prefix(shard, axis, join, neutral, backward):
    count = lax.axis_size(axis)
    place = lax.axis_index(axis)
    ahead = count - 1 - place if backward else place
    gathered = jax.tree.map(
        lambda a, kind: lax.all_gather(a.astype(kind), axis), shard, (jnp.bfloat16, jnp.bfloat16)
    )
    state = jax.tree.map(lambda a, e: jnp.zeros_like(a) + jnp.asarray(e, a.dtype), shard, neutral)

    def one(lap, state):
        source = count - 1 - lap if backward else lap
        return join(
            state,
            jax.tree.map(
                lambda a, own: lax.dynamic_index_in_dim(a, source, 0, False).astype(own.dtype),
                gathered,
                shard,
            ),
        )

    return lax.fori_loop(0, ahead, one, state)


def feature_pair(logits):
    plus_half = jax.nn.softmax(logits, axis=-1)
    minus_half = jax.nn.softmax(-logits, axis=-1)
    return (plus_half, minus_half)


def pair_backward(plus_half, minus_half, d_features):
    feat_count = plus_half.shape[-1]
    d_plus = d_features[..., :feat_count]
    d_minus = d_features[..., feat_count:]
    inner_plus = jnp.sum(d_plus * plus_half, axis=-1, keepdims=True)
    inner_minus = jnp.sum(d_minus * minus_half, axis=-1, keepdims=True)
    return plus_half * (d_plus - inner_plus) - minus_half * (d_minus - inner_minus)


def add_pair(earlier_pair, later_pair):
    return (earlier_pair[0] + later_pair[0], earlier_pair[1] + later_pair[1])


def attend(running, row_block, query_pos, key_view, value_view, key_pos, score_scale):
    row_max, row_sum, weighted = running
    scores = (
        jnp.einsum("rkgd,lkd->kgrl", row_block, key_view, preferred_element_type=jnp.float32)
        * score_scale
    )
    visible = key_pos[None, None, None, :] <= query_pos[None, None, :, None]
    masked = jnp.where(visible, scores, NEG_LARGE)
    new_max = jnp.maximum(row_max, jnp.max(masked, axis=-1))
    exponent = jnp.where(visible, jnp.exp(masked - new_max[..., None]), 0.0)
    weights = exponent.astype(jnp.bfloat16)
    weighted = jnp.einsum("kgrl,lkd->kgrd", weights, value_view, preferred_element_type=jnp.float32)
    row_sum = jnp.sum(exponent, axis=-1)
    return (new_max, row_sum, weighted)


def local(queries, key_matrix, value_matrix, query_feature_weight, key_feature_weight):
    token_rows = queries.shape[0]
    local_heads = key_matrix.shape[1] // HEAD_SIZE
    seq_count = lax.axis_size("seq")
    position = lax.axis_index("seq")
    first_row = position * token_rows
    seg_total = token_rows * seq_count
    score_scale = HEAD_SIZE ** (-0.5)
    query_heads = queries.reshape(token_rows, local_heads, GROUP_QUERIES, HEAD_SIZE)
    key_heads = key_matrix.reshape(token_rows, local_heads, HEAD_SIZE)
    value_heads = value_matrix.reshape(token_rows, local_heads, HEAD_SIZE)
    query_map_view = query_feature_weight.reshape(
        HEAD_SIZE, local_heads, GROUP_QUERIES, HALF_FEATURES
    )
    key_map_view = key_feature_weight.reshape(HEAD_SIZE, local_heads, HALF_FEATURES)
    query_sets = ((query_heads, first_row + jnp.arange(token_rows, dtype=jnp.int32)),)

    def fresh_carry(row_block):
        row_count = row_block.shape[0]
        return (
            jnp.full((local_heads, GROUP_QUERIES, row_count), NEG_LARGE, jnp.float32),
            jnp.zeros((local_heads, GROUP_QUERIES, row_count), jnp.float32),
            jnp.zeros((local_heads, GROUP_QUERIES, row_count, HEAD_SIZE), jnp.float32),
        )

    first_key = jnp.int32(0)
    key_block = lax.all_gather(key_matrix, "seq", axis=0, tiled=True)
    value_block = lax.all_gather(value_matrix, "seq", axis=0, tiled=True)
    key_count = key_block.shape[0]
    key_view = key_block.reshape(key_count, local_heads, HEAD_SIZE)
    value_view = value_block.reshape(key_count, local_heads, HEAD_SIZE)
    key_pos = jnp.arange(key_count, dtype=jnp.int32)
    teach_runs = tuple((fresh_carry(query_set[0]) for query_set in query_sets))
    updated = []
    for query_set, fold_teach_run in zip(query_sets, teach_runs):
        row_block, query_pos = query_set

        def visit_block(current, row_block=row_block, query_pos=query_pos):
            return attend(current, row_block, query_pos, key_view, value_view, key_pos, score_scale)

        def unchanged(current):
            return current

        updated.append(lax.cond(first_key <= query_pos[-1], visit_block, unchanged, fold_teach_run))
    teach_done = tuple(updated)

    def finish(teach_run):
        return (teach_run[2] / teach_run[1][..., None]).astype(jnp.bfloat16)

    finished = [finish(teach_run) for teach_run in teach_done]
    teacher = finished[0]
    query_logits = jnp.einsum(
        "tkgd,dkgf->kgtf", query_heads, query_map_view, preferred_element_type=jnp.float32
    )
    query_plus, query_minus = feature_pair(query_logits)
    query_phi = jnp.concatenate([query_plus, query_minus], axis=-1).astype(jnp.bfloat16)
    logits = jnp.einsum("lkd,dkf->klf", key_heads, key_map_view, preferred_element_type=jnp.float32)
    plus_half, minus_half = feature_pair(logits)
    key_phi = jnp.concatenate([plus_half, minus_half], axis=-1).astype(jnp.bfloat16)
    block_state = jnp.einsum(
        "ktf,tkd->kfd", key_phi, value_heads, preferred_element_type=jnp.float32
    )
    block_norm = jnp.sum(key_phi.astype(jnp.float32), axis=1)
    zero_pair = (jnp.zeros_like(block_state), jnp.zeros_like(block_norm))
    prefix_state, prefix_norm = prefix((block_state, block_norm), "seq", add_pair, zero_pair, False)
    prefix_low = prefix_state.astype(jnp.bfloat16)
    token_index = jnp.arange(token_rows, dtype=jnp.int32)
    causal = token_index[None, :] <= token_index[:, None]
    intra_scores = jnp.where(
        causal,
        jnp.einsum("kgtf,ksf->kgts", query_phi, key_phi, preferred_element_type=jnp.float32),
        0.0,
    )
    numerator = jnp.einsum(
        "kgts,skd->kgtd",
        intra_scores.astype(jnp.bfloat16),
        value_heads,
        preferred_element_type=jnp.float32,
    )
    numerator = numerator + jnp.einsum(
        "kgtf,kfd->kgtd", query_phi, prefix_low, preferred_element_type=jnp.float32
    )
    query_wide = query_phi.astype(jnp.float32)
    denominator = jnp.sum(intra_scores, axis=-1) + jnp.einsum(
        "kgtf,kf->kgt", query_wide, prefix_norm, precision=lax.Precision.HIGHEST
    )
    student = numerator / denominator[..., None]
    target = teacher.astype(jnp.float32)
    differ = student - target
    loss_local = jnp.sum(differ * differ)
    grad_out = 2.0 * differ / seg_total
    numer_grad = grad_out / denominator[..., None]
    denom_grad = -jnp.sum(grad_out * student, axis=-1) / denominator
    numer_low = numer_grad.astype(jnp.bfloat16)
    coupling = (
        jnp.einsum("kgtd,skd->kgts", numer_low, value_heads, preferred_element_type=jnp.float32)
        + denom_grad[..., None]
    )
    coupling_low = jnp.where(causal, coupling, 0.0).astype(jnp.bfloat16)
    later_state = jnp.einsum(
        "kgtf,kgtd->kfd", query_phi, numer_low, preferred_element_type=jnp.float32
    )
    later_norm = jnp.einsum("kgtf,kgt->kf", query_wide, denom_grad, precision=lax.Precision.HIGHEST)
    zero_later = (jnp.zeros_like(later_state), jnp.zeros_like(later_norm))
    suffix_state, suffix_norm = prefix((later_state, later_norm), "seq", add_pair, zero_later, True)
    suffix_low = suffix_state.astype(jnp.bfloat16)
    query_dphi = jnp.einsum(
        "kgts,ksf->kgtf", coupling_low, key_phi, preferred_element_type=jnp.float32
    )
    query_dphi = query_dphi + jnp.einsum(
        "kgtd,kfd->kgtf", numer_low, prefix_low, preferred_element_type=jnp.float32
    )
    query_dphi = query_dphi + denom_grad[..., None] * prefix_norm[:, None, None, :]
    key_dphi = jnp.einsum(
        "kgts,kgtf->ksf", coupling_low, query_phi, preferred_element_type=jnp.float32
    )
    key_dphi = key_dphi + jnp.einsum(
        "skd,kfd->ksf", value_heads, suffix_low, preferred_element_type=jnp.float32
    )
    key_dphi = key_dphi + suffix_norm[:, None, :]
    query_dlogit = pair_backward(query_plus, query_minus, query_dphi).astype(jnp.bfloat16)
    key_dlogit = pair_backward(plus_half, minus_half, key_dphi).astype(jnp.bfloat16)
    query_grad = jnp.einsum(
        "tkgd,kgtf->dkgf", query_heads, query_dlogit, preferred_element_type=jnp.float32
    )
    key_grad = jnp.einsum("tkd,ktf->dkf", key_heads, key_dlogit, preferred_element_type=jnp.float32)
    query_grad, key_grad = lax.psum((query_grad, key_grad), "seq")
    transfer_loss = lax.psum(loss_local, ("seq", "head")) / seg_total
    student_out = (
        student.astype(jnp.bfloat16)
        .transpose(2, 0, 1, 3)
        .reshape(token_rows, local_heads * GROUP_QUERIES * HEAD_SIZE)
    )
    return (
        student_out,
        query_grad.reshape(HEAD_SIZE, local_heads * GROUP_QUERIES * HALF_FEATURES),
        key_grad.reshape(HEAD_SIZE, local_heads * HALF_FEATURES),
        transfer_loss,
    )


def solution(mesh):
    placed = (
        P("seq", "head"),
        P("seq", "head"),
        P("seq", "head"),
        P(None, "head"),
        P(None, "head"),
    )
    return jax.shard_map(
        local,
        mesh=mesh,
        in_specs=placed,
        out_specs=(P("seq", "head"), P(None, "head"), P(None, "head"), P()),
        check_vma=False,
    )
```

profile of v0, /device:TPU:2, one launch (start us, length us, event | category | flops | bytes accessed | tf_op | source)
XLA Modules:
  0.0 812.8 jit_solution(13775298181172924217)
XLA Ops:
  7.9 0.9 fusion.99
  8.9 1.5 convolution_convert_fusion
  13.4 1.0 copy.51
  14.5 49.8 %all-gather.4 = bf16[64,1,128]{2,1,0:T(2,128)(2,1)S(1)} all-gather(bf16[1,1,128]{2,1,0:T(2,128)(2,1)S(1)} %bitcast.271), channel_id=3, replica_groups=mesh['seq'=64,'head'=8] {'seq'}, dimensions={0}, use_global_device_ids=true | all-gather | bytes 16640 | tf_op jit(solution)/shard_map/all_gather | solution.py:17
  64.3 1.3 fusion.103
  65.7 1.3 fusion.100
  67.5 1.1 fusion.38
  68.7 31.2 %all-gather.15.cloned.1.call-done = bf16[8192,128]{1,0:T(8,128)(2,1)} async-done(((bf16[128,128]{1,0:T(8,128)(2,1)}), bf16[8192,128]{1,0:T(8,128)(2,1)}) %all-gather.15.cloned.1.call-update) | async-done | bytes 2097168 | tf_op jit(solution)/shard_map/all_gather | solution.py:17
  100.2 83.5 %all-gather.11.cloned.1.call-done = bf16[9216,128]{1,0:T(8,128)(2,1)} async-done(((bf16[144,128]{1,0:T(8,128)(2,1)}), bf16[9216,128]{1,0:T(8,128)(2,1)}) %all-gather.11.cloned.1.call-update) | async-done | bytes 2359312 | tf_op jit(solution)/shard_map/all_gather | solution.py:96
  183.7 83.7 %all-gather.13.cloned.1.call-done = bf16[9216,128]{1,0:T(8,128)(2,1)} async-done(((bf16[144,128]{1,0:T(8,128)(2,1)}), bf16[9216,128]{1,0:T(8,128)(2,1)}) %all-gather.13.cloned.1.call-update) | async-done | bytes 2359312 | tf_op jit(solution)/shard_map/all_gather | solution.py:97
  267.4 62.5 %conditional.1 = (f32[1,8,144]{2,1,0:T(8,128)}, f32[1,8,144,128]{3,2,1,0:T(8,128)}) conditional(s32[]{:T(128)} %bitcast.28, () %tuple.33, (s32[9216]{0:T(1024)S(1)}, s32[144]{0:T(256)}, bf16[144,1024]{1,0:T(8,128)(2,1)}, bf16[9216,128]{1,0:T(8,128)(2,1)}, bf16[9216,128]{1,0:T(8,128)(2,1)}) %tuple.98), branch_computations={%region_12.13_spmd, %region_13.16_spmd} | conditional | flops 5575162880 | bytes 138378832 | solution.py:113
  267.6 1.4 broadcast_compare_fusion
  269.0 18.7 %fusion = (f32[8,144]{1,0:T(8,128)S(1)}, f32[9216,144,8]{0,1,2:T(8,128)}) fusion(pred[144,9216]{1,0:T(8,128)(4,1)S(1)} %broadcast_compare_fusion, bf16[9216,128]{1,0:T(8,128)(2,1)} %get-tuple-element.118, bf16[144,1024]{1,0:T(8,128)(2,1)} %get-tuple-element.119), kind=kOutput, calls=%fused_computation.4 | convolution fusion | flops 2749758464 | bytes 46453248 | tf_op jit(solution)/shard_map/cond/branch_1_fun/rkgd,lkd->kgrl/dot_general | solution.py:57
  287.7 21.9 %fusion.2 = f32[8,144]{1,0:T(8,128)} fusion(f32[9216,144,8]{0,1,2:T(8,128)} %get-tuple-element.217, f32[8,144]{1,0:T(8,128)S(1)} %broadcast_maximum_fusion, pred[144,9216]{1,0:T(8,128)(4,1)S(1)} %broadcast_compare_fusion), kind=kLoop, calls=%fused_computation.6 | loop fusion | flops 53083008 | bytes 43803648 | tf_op jit(solution)/shard_map/cond/branch_1_fun/reduce_sum | solution.py:66
  309.6 20.2 %fusion.10 = f32[1,8,144,128]{3,2,1,0:T(8,128)} fusion(bf16[9216,128]{1,0:T(8,128)(2,1)} %get-tuple-element.120, f32[9216,144,8]{0,1,2:T(8,128)} %get-tuple-element.217, f32[8,144]{1,0:T(8,128)S(1)} %broadcast_maximum_fusion, pred[144,9216]{1,0:T(8,128)(4,1)S(1)} %broadcast_compare_fusion), kind=kOutput, calls=%fused_computation.14 | convolution fusion | flops 2770993152 | bytes 46748160 | tf_op jit(solution)/shard_map/cond/branch_1_fun/kgrl,lkd->kgrd/dot_general | solution.py:65
  329.9 2.8 multiply_reduce_fusion
  332.9 1.9 fusion.34
  334.9 95.5 %psum.23 = f32[]{:T(128)} all-reduce(f32[]{:T(128)} %get-tuple-element.183), channel_id=1, replica_groups=mesh['seq'=64,'head'=8] {'seq','head'}, use_global_device_ids=true, to_apply=%region_26.27 | all-reduce | flops 1 | bytes 8 | tf_op jit(solution)/shard_map/psum | solution.py:197
  432.8 0.8 copy.65
  434.1 42.6 %all-gather.5 = bf16[64,1,128]{2,1,0:T(2,128)(2,1)S(1)} all-gather(bf16[1,1,128]{2,1,0:T(2,128)(2,1)S(1)} %fusion.36), channel_id=5, replica_groups=mesh['seq'=64,'head'=8] {'seq'}, dimensions={0}, use_global_device_ids=true | all-gather | bytes 16640 | tf_op jit(solution)/shard_map/all_gather | solution.py:17
  477.8 51.3 %while.27 = (s32[]{:T(128)}, f32[1,128,128]{2,1,0:T(8,128)S(1)}, f32[1,128]{1,0:T(1,128)S(1)}, s32[]{:T(128)}, bf16[64,1,128,128]{3,2,1,0:T(8,128)(2,1)}, /*inde...) while((s32[]{:T(128)}, f32[1,128,128]{2,1,0:T(8,128)S(1)}, ...), condition=%wide.region_21.22_spmd, body=%wide.region_20.21_spmd.sunk | while | flops 33030 | bytes 165283 | solution.py:32
  483.5 0.8 convert_add_fusion.10
  484.3 0.8 convert_add_fusion.10
  490.0 0.8 convert_add_fusion.10
  490.8 0.8 convert_add_fusion.10
  494.9 0.8 convert_add_fusion.10
  495.7 0.8 convert_add_fusion.10
  498.2 0.8 convert_add_fusion.10
  499.0 0.8 convert_add_fusion.10
  501.4 0.8 convert_add_fusion.10
  529.5 274.0 %psum.22 = f32[128,64]{0,1:T(8,128)} all-reduce(f32[128,64]{0,1:T(8,128)S(1)} %convolution_bitcast_fusion.3), channel_id=1, replica_groups=mesh['seq'=64,'head'=8] {'seq'}, use_global_device_ids=true, to_apply=%region_24.25 | all-reduce | flops 8192 | bytes 65536 | tf_op jit(solution)/shard_map/psum | solution.py:196
  803.5 1.7 copy.144
  (187 shorter events, 50.6 us)
Async XLA Ops:
  7.2 0.7 copy-start
  7.2 92.6 %all-gather.15.cloned.1.call-start = ((), (), s32[]{:S(2)}) async-start(), calls=%async_computation.3 | async-start | bytes 2129920 | tf_op jit(solution)/shard_map/all_gather | solution.py:17
  8.8 4.5 copy-start.5
  8.9 4.4 copy-start.7
  8.9 4.4 copy-start.9
  10.5 173.1 %all-gather.11.cloned.1.call-start = ((), (), s32[]{:S(2)}) async-start(), calls=%async_computation | async-start | bytes 2396160 | tf_op jit(solution)/shard_map/all_gather | solution.py:96
  11.3 256.1 %all-gather.13.cloned.1.call-start = ((), (), s32[]{:S(2)}) async-start(), calls=%async_computation.1 | async-start | bytes 2396160 | tf_op jit(solution)/shard_map/all_gather | solution.py:97
  12.0 465.7 %all-gather.17.cloned.1.call-start = ((), (), s32[]{:S(2)}) async-start(), calls=%async_computation.4 | async-start | bytes 2129920 | tf_op jit(solution)/shard_map/all_gather | solution.py:17
  12.1 1.3 copy-start.11
  67.1 200.2 %copy-start.2 = (bf16[8,144,64]{1,2,0:T(8,128)(2,1)}, bf16[8,144,64]{1,2,0:T(8,128)(2,1)S(1)}, u32[]{:S(2)}) copy-start(bf16[8,144,64]{1,2,0:T(8,128)(2,1)S(1)} %get-tuple-element.233) | copy-start | bytes 442372
  267.4 163.9 %copy-start.1 = (bf16[144,128]{1,0:T(8,128)(2,1)S(1)}, bf16[144,128]{1,0:T(8,128)(2,1)}, u32[]{:S(2)}) copy-start(bf16[144,128]{1,0:T(8,128)(2,1)} %param.13) | copy-start | bytes 110596
  329.9 102.6 %copy-start.12 = (bf16[144,1024]{1,0:T(8,128)(2,1)S(1)}, bf16[144,1024]{1,0:T(8,128)(2,1)}, u32[]{:S(2)}) copy-start(bf16[144,1024]{1,0:T(8,128)(2,1)} %param.11) | copy-start | bytes 884740
  329.9 103.8 %copy-start.3 = (bf16[8,144,64]{1,2,0:T(8,128)(2,1)S(1)}, bf16[8,144,64]{1,2,0:T(8,128)(2,1)}, u32[]{:S(2)}) copy-start(bf16[8,144,64]{1,2,0:T(8,128)(2,1)} %copy-done.2) | copy-start | bytes 442372
  332.7 196.6 %copy-start.6 = (f32[144]{0:T(256)S(1)}, f32[144]{0:T(256)}, u32[]{:S(2)}) copy-start(f32[144]{0:T(256)} %copy-done.5) | copy-start | bytes 1732
  332.7 196.6 %copy-start.8 = (f32[144]{0:T(256)S(1)}, f32[144]{0:T(256)}, u32[]{:S(2)}) copy-start(f32[144]{0:T(256)} %copy-done.7) | copy-start | bytes 1732
  332.7 196.6 %copy-start.10 = (f32[144]{0:T(256)S(1)}, f32[144]{0:T(256)}, u32[]{:S(2)}) copy-start(f32[144]{0:T(256)} %copy-done.9) | copy-start | bytes 1732
  332.9 196.5 %copy-start.4 = (bf16[144,128]{1,0:T(8,128)(2,1)S(1)}, bf16[144,128]{1,0:T(8,128)(2,1)}, u32[]{:S(2)}) copy-start(bf16[144,128]{1,0:T(8,128)(2,1)} %param.12) | copy-start | bytes 110596
  334.8 468.7 %all-reduce.2.cloned.1.call-start = ((), (), s32[]{:S(2)}) async-start(), calls=%async_computation.2 | async-start | bytes 524288 | tf_op jit(solution)/shard_map/psum | solution.py:196
Sparse Core Ops, SparseCore 0:
  11.6 88.1 all-gather.14
  102.9 80.7 all-gather.10
  186.7 80.5 all-gather.12
  334.9 80.1 all-gather.16
  477.2 147.5 all-reduce.1
where the time goes:
time: 818 us; the launch traced here: 813 us
  blocking collectives  462 us (56%)
  waiting for transfers between devices  200 us (24%)
  other arithmetic  73.9 us (9%)
  matrix products  53 us (6%)
  between operations  16.5 us (2%)
    psum x1, blocking collectives, local(): query_grad, key_grad = lax.psum((query_grad, key_grad), 'seq')  274 us
    psum x1, blocking collectives, local(): transfer_loss = lax.psum(loss_local, ('seq', 'head')) / seg_total  95.5 us
    all_gather x2, blocking collectives, prefix(): lax.all_gather(a.astype(kind), axis)  92.4 us
    all_gather x1, waiting for transfers between devices, local(): value_block = lax.all_gather(value_matrix, 'seq', axis=0, tiled=True)  83.7 us
    all_gather x1, waiting for transfers between devices, local(): key_block = lax.all_gather(key_matrix, 'seq', axis=0, tiled=True)  83.5 us
    add x126, other arithmetic, add_pair(): return (earlier_pair[0] + later_pair[0], earlier_pair[1] + later_pair[1])  49.7 us
    all_gather x2, waiting for transfers between devices, prefix(): lax.all_gather(a.astype(kind), axis)  31.2 us
    reduce_sum x1, other arithmetic, attend(): row_sum = jnp.sum(exponent, axis=-1)  21.9 us
  transfers between devices with their start and end apart: 5, of which 3 were waited for; matrix products, arithmetic and copies ran while one was open for 7% of the time, Pallas kernels for 0%

commit v1 on v0

--- a/solution.py
+++ b/solution.py
@@ -94,7 +94,9 @@
 
     first_key = jnp.int32(0)
     key_block = lax.all_gather(key_matrix, "seq", axis=0, tiled=True)
-    value_block = lax.all_gather(value_matrix, "seq", axis=0, tiled=True)
+    value_block = jnp.concatenate(
+        lax.all_to_all(jnp.stack([value_matrix] * lax.axis_size("seq")), "seq", 0, 0), axis=0
+    )
     key_count = key_block.shape[0]
     key_view = key_block.reshape(key_count, local_heads, HEAD_SIZE)
     value_view = value_block.reshape(key_count, local_heads, HEAD_SIZE)

time: 818 us -> 782 us (0.956)
  waiting for transfers between devices: 200 us -> 104 us
  blocking collectives: 462 us -> 503 us
  starting transfers between devices: 0.2 us -> 17 us
    all_gather x1 -> x0, waiting for transfers between devices: 83.7 us -> none  [local(): value_block = lax.all_gather(value_matrix, 'seq', axis=0, tiled=True)]
    all_gather x2, blocking collectives: 92.4 us -> 134 us  [prefix(): lax.all_gather(a.astype(kind), axis)]
    all_to_all x0 -> x1, starting transfers between devices: none -> 16.8 us  [local(): lax.all_to_all(jnp.stack([value_matrix] * lax.axis_size('seq')), 'seq', 0...]
    all_gather x2, waiting for transfers between devices: 31.2 us -> 19.6 us  [prefix(): lax.all_gather(a.astype(kind), axis)]
  transfers between devices with their start and end apart: 5 -> 5, of which waited for: 3 -> 2; matrix products, arithmetic and copies ran while one was open for 7% -> 8% of each run, Pallas kernels for 0% -> 0%
where the time goes in v1:
time: 782 us; the launch traced here: 777 us
  blocking collectives  503 us (64%)
  waiting for transfers between devices  104 us (13%)
  other arithmetic  74.2 us (9%)
  matrix products  52.2 us (7%)
  starting transfers between devices  17 us (2%)
  between operations  16.5 us (2%)
  local copies, waits for them, and re-layouts  8.18 us (1%)
    psum x1, blocking collectives, local(): query_grad, key_grad = lax.psum((query_grad, key_grad), 'seq')  274 us
    all_gather x2, blocking collectives, prefix(): lax.all_gather(a.astype(kind), axis)  134 us
    psum x1, blocking collectives, local(): transfer_loss = lax.psum(loss_local, ('seq', 'head')) / seg_total  95.5 us
    all_gather x1, waiting for transfers between devices, local(): key_block = lax.all_gather(key_matrix, 'seq', axis=0, tiled=True)  83.6 us
    add x126, other arithmetic, add_pair(): return (earlier_pair[0] + later_pair[0], earlier_pair[1] + later_pair[1])  50 us
    reduce_sum x1, other arithmetic, attend(): row_sum = jnp.sum(exponent, axis=-1)  21.9 us
    dot_general x1, matrix products, attend(): jnp.einsum('kgrl,lkd->kgrd', weights, value_view, preferred_element_type=...  20.2 us
    all_gather x2, waiting for transfers between devices, prefix(): lax.all_gather(a.astype(kind), axis)  19.6 us
  transfers between devices with their start and end apart: 5, of which 2 were waited for; matrix products, arithmetic and copies ran while one was open for 8% of the time, Pallas kernels for 0%

profile of v1, /device:TPU:2, one launch (start us, length us, event | category | flops | bytes accessed | tf_op | source)
XLA Modules:
  0.0 777.1 jit_solution(14545461984367511052)
XLA Ops:
  7.9 0.9 fusion.96
  8.9 1.5 convolution_convert_fusion
  11.3 2.5 stack.2
  13.8 16.8 %all-to-all-start = ((bf16[64,144,128]{2,1,0:T(8,128)(2,1)}), bf16[64,144,128]{2,1,0:T(8,128)(2,1)}, u32[]{:S(2)}, u32[]{:S(2)}) async-start(bf16[64,144,128]{2,1,0:T(8,128)(2,1)} %stack.2), calls=%async_computation | async-start | bytes 4718592 | tf_op jit(solution)/shard_map/all_to_all | solution.py:98
  31.9 1.0 copy.51
  33.1 91.3 %all-gather.4 = bf16[64,1,128]{2,1,0:T(2,128)(2,1)S(1)} all-gather(bf16[1,1,128]{2,1,0:T(2,128)(2,1)S(1)} %bitcast.270), channel_id=3, replica_groups=mesh['seq'=64,'head'=8] {'seq'}, dimensions={0}, use_global_device_ids=true | all-gather | bytes 16640 | tf_op jit(solution)/shard_map/all_gather | solution.py:17
  124.4 1.3 fusion.100
  125.7 1.3 fusion.97
  128.0 19.6 %all-gather.12.cloned.1.call-done = bf16[8192,128]{1,0:T(8,128)(2,1)} async-done(((bf16[128,128]{1,0:T(8,128)(2,1)}), bf16[8192,128]{1,0:T(8,128)(2,1)}) %all-gather.12.cloned.1.call-update) | async-done | bytes 2097168 | tf_op jit(solution)/shard_map/all_gather | solution.py:17
  147.9 83.6 %all-gather.10.cloned.1.call-done = bf16[9216,128]{1,0:T(8,128)(2,1)} async-done(((bf16[144,128]{1,0:T(8,128)(2,1)}), bf16[9216,128]{1,0:T(8,128)(2,1)}) %all-gather.10.cloned.1.call-update) | async-done | bytes 2359312 | tf_op jit(solution)/shard_map/all_gather | solution.py:96
  231.5 62.5 %conditional.1 = (f32[1,8,144]{2,1,0:T(8,128)}, f32[1,8,144,128]{3,2,1,0:T(8,128)}) conditional(s32[]{:T(128)} %bitcast.29, () %tuple.33, (s32[9216]{0:T(1024)S(1)}, s32[144]{0:T(256)}, bf16[144,1024]{1,0:T(8,128)(2,1)}, bf16[9216,128]{1,0:T(8,128)(2,1)}, bf16[64,144,128]{2,1,0:T(8,128)(2,1)}) %tuple.96), branch_computations={%region_12.13_spmd, %region_13.16_spmd} | conditional | flops 5575162880 | bytes 138378832 | solution.py:115
  231.7 1.4 broadcast_compare_fusion
  233.2 18.7 %fusion = (f32[8,144]{1,0:T(8,128)S(1)}, f32[9216,144,8]{0,1,2:T(8,128)}) fusion(pred[144,9216]{1,0:T(8,128)(4,1)S(1)} %broadcast_compare_fusion, bf16[9216,128]{1,0:T(8,128)(2,1)} %get-tuple-element.118, bf16[144,1024]{1,0:T(8,128)(2,1)} %get-tuple-element.119), kind=kOutput, calls=%fused_computation.4 | convolution fusion | flops 2749758464 | bytes 46453248 | tf_op jit(solution)/shard_map/cond/branch_1_fun/rkgd,lkd->kgrl/dot_general | solution.py:57
  251.9 21.9 %fusion.2 = f32[8,144]{1,0:T(8,128)} fusion(f32[9216,144,8]{0,1,2:T(8,128)} %get-tuple-element.217, f32[8,144]{1,0:T(8,128)S(1)} %broadcast_maximum_fusion, pred[144,9216]{1,0:T(8,128)(4,1)S(1)} %broadcast_compare_fusion), kind=kLoop, calls=%fused_computation.6 | loop fusion | flops 53083008 | bytes 43803648 | tf_op jit(solution)/shard_map/cond/branch_1_fun/reduce_sum | solution.py:66
  273.8 20.2 %fusion.9 = f32[1,8,144,128]{3,2,1,0:T(8,128)} fusion(bf16[9216,128,1]{1,0,2:T(8,128)(2,1)} %bitcast.8, f32[9216,144,8]{0,1,2:T(8,128)} %get-tuple-element.217, f32[8,144]{1,0:T(8,128)S(1)} %broadcast_maximum_fusion, pred[144,9216]{1,0:T(8,128)(4,1)S(1)} %broadcast_compare_fusion), kind=kOutput, calls=%fused_computation.13 | convolution fusion | flops 2770993152 | bytes 46748160 | tf_op jit(solution)/shard_map/cond/branch_1_fun/kgrl,lkd->kgrd/dot_general | solution.py:65
  294.0 2.8 multiply_reduce_fusion
  297.1 1.9 fusion.31
  299.0 95.5 %psum.23 = f32[]{:T(128)} all-reduce(f32[]{:T(128)} %get-tuple-element.183), channel_id=1, replica_groups=mesh['seq'=64,'head'=8] {'seq','head'}, use_global_device_ids=true, to_apply=%region_26.27 | all-reduce | flops 1 | bytes 8 | tf_op jit(solution)/shard_map/psum | solution.py:199
  396.9 0.8 copy.65
  398.2 42.5 %all-gather.5 = bf16[64,1,128]{2,1,0:T(2,128)(2,1)S(1)} all-gather(bf16[1,1,128]{2,1,0:T(2,128)(2,1)S(1)} %fusion.33), channel_id=5, replica_groups=mesh['seq'=64,'head'=8] {'seq'}, dimensions={0}, use_global_device_ids=true | all-gather | bytes 16640 | tf_op jit(solution)/shard_map/all_gather | solution.py:17
  441.9 51.5 %while.27 = (s32[]{:T(128)}, f32[1,128,128]{2,1,0:T(8,128)S(1)}, f32[1,128]{1,0:T(1,128)S(1)}, s32[]{:T(128)}, bf16[64,1,128,128]{3,2,1,0:T(8,128)(2,1)}, /*inde...) while((s32[]{:T(128)}, f32[1,128,128]{2,1,0:T(8,128)S(1)}, ...), condition=%wide.region_21.22_spmd, body=%wide.region_20.21_spmd.sunk | while | flops 33030 | bytes 165283 | solution.py:32
  447.6 0.8 convert_add_fusion.10
  448.4 0.8 convert_add_fusion.10
  454.1 0.8 convert_add_fusion.10
  458.2 0.8 convert_add_fusion.10
  459.0 0.8 convert_add_fusion.10
  459.8 0.8 convert_add_fusion.10
  461.5 0.8 convert_add_fusion.10
  462.3 0.8 convert_add_fusion.10
  464.8 0.8 convert_add_fusion.10
  493.8 274.0 %psum.22 = f32[128,64]{0,1:T(8,128)} all-reduce(f32[128,64]{0,1:T(8,128)S(1)} %convolution_bitcast_fusion.3), channel_id=1, replica_groups=mesh['seq'=64,'head'=8] {'seq'}, use_global_device_ids=true, to_apply=%region_24.25 | all-reduce | flops 8192 | bytes 65536 | tf_op jit(solution)/shard_map/psum | solution.py:198
  767.7 1.7 copy.144
  (187 shorter events, 50.5 us)
Async XLA Ops:
  7.2 0.7 copy-start
  7.2 120.4 %copy-start.1 = (bf16[144,128]{1,0:T(8,128)(2,1)S(1)}, bf16[144,128]{1,0:T(8,128)(2,1)}, u32[]{:S(2)}) copy-start(bf16[144,128]{1,0:T(8,128)(2,1)} %param.13) | copy-start | bytes 110596
  7.2 140.4 %all-gather.12.cloned.1.call-start = ((), (), s32[]{:S(2)}) async-start(), calls=%async_computation.3 | async-start | bytes 2129920 | tf_op jit(solution)/shard_map/all_gather | solution.py:17
  8.8 23.1 %copy-start.5 = (f32[144]{0:T(256)}, f32[144]{0:T(256)S(1)}, u32[]{:S(2)}) copy-start(f32[144]{0:T(256)S(1)} %get-tuple-element.190) | copy-start | bytes 1732
  8.9 23.0 %copy-start.7 = (f32[144]{0:T(256)}, f32[144]{0:T(256)S(1)}, u32[]{:S(2)}) copy-start(f32[144]{0:T(256)S(1)} %get-tuple-element.187) | copy-start | bytes 1732
  8.9 23.0 %copy-start.9 = (f32[144]{0:T(256)}, f32[144]{0:T(256)S(1)}, u32[]{:S(2)}) copy-start(f32[144]{0:T(256)S(1)} %get-tuple-element.188) | copy-start | bytes 1732
  10.5 221.0 %all-gather.10.cloned.1.call-start = ((), (), s32[]{:S(2)}) async-start(), calls=%async_computation.1 | async-start | bytes 2396160 | tf_op jit(solution)/shard_map/all_gather | solution.py:96
  13.8 217.8 %all-to-all-start = ((bf16[64,144,128]{2,1,0:T(8,128)(2,1)}), bf16[64,144,128]{2,1,0:T(8,128)(2,1)}, u32[]{:S(2)}, u32[]{:S(2)}) async-start(bf16[64,144,128]{2,1,0:T(8,128)(2,1)} %stack.2), calls=%async_computation | async-start | bytes 4718592 | tf_op jit(solution)/shard_map/all_to_all | solution.py:98
  30.6 411.2 %all-gather.14.cloned.1.call-start = ((), (), s32[]{:S(2)}) async-start(), calls=%async_computation.4 | async-start | bytes 2129920 | tf_op jit(solution)/shard_map/all_gather | solution.py:17
  30.6 1.3 copy-start.11
  127.2 104.3 %copy-start.2 = (bf16[8,144,64]{1,2,0:T(8,128)(2,1)}, bf16[8,144,64]{1,2,0:T(8,128)(2,1)S(1)}, u32[]{:S(2)}) copy-start(bf16[8,144,64]{1,2,0:T(8,128)(2,1)S(1)} %get-tuple-element.233) | copy-start | bytes 442372
  294.0 102.6 %copy-start.12 = (bf16[144,1024]{1,0:T(8,128)(2,1)S(1)}, bf16[144,1024]{1,0:T(8,128)(2,1)}, u32[]{:S(2)}) copy-start(bf16[144,1024]{1,0:T(8,128)(2,1)} %param.11) | copy-start | bytes 884740
  294.0 103.7 %copy-start.3 = (bf16[8,144,64]{1,2,0:T(8,128)(2,1)S(1)}, bf16[8,144,64]{1,2,0:T(8,128)(2,1)}, u32[]{:S(2)}) copy-start(bf16[8,144,64]{1,2,0:T(8,128)(2,1)} %copy-done.2) | copy-start | bytes 442372
  296.8 196.7 %copy-start.6 = (f32[144]{0:T(256)S(1)}, f32[144]{0:T(256)}, u32[]{:S(2)}) copy-start(f32[144]{0:T(256)} %copy-done.5) | copy-start | bytes 1732
  296.8 196.7 %copy-start.8 = (f32[144]{0:T(256)S(1)}, f32[144]{0:T(256)}, u32[]{:S(2)}) copy-start(f32[144]{0:T(256)} %copy-done.7) | copy-start | bytes 1732
  296.8 196.7 %copy-start.10 = (f32[144]{0:T(256)S(1)}, f32[144]{0:T(256)}, u32[]{:S(2)}) copy-start(f32[144]{0:T(256)} %copy-done.9) | copy-start | bytes 1732
  297.0 196.6 %copy-start.4 = (bf16[144,128]{1,0:T(8,128)(2,1)S(1)}, bf16[144,128]{1,0:T(8,128)(2,1)}, u32[]{:S(2)}) copy-start(bf16[144,128]{1,0:T(8,128)(2,1)} %param.12) | copy-start | bytes 110596
  299.0 468.8 %all-reduce.2.cloned.1.call-start = ((), (), s32[]{:S(2)}) async-start(), calls=%async_computation.2 | async-start | bytes 524288 | tf_op jit(solution)/shard_map/psum | solution.py:198
Sparse Core Ops, SparseCore 0:
  11.6 135.8 all-gather.11
  150.6 80.8 all-gather.9
  299.1 80.1 all-gather.13
  441.3 147.4 all-reduce.1
